TPU v7x, 512 devices: a whole 4x4x16 slice. The times are simulated.
512 devices in a mesh: tm: 8 (over y, core), net: 16 (over z), cols: 4 (over x).
Axes of the slice: x: 4, y: 4, z: 16, core: 2. Of those that a mesh axis runs over, the one named last changes fastest.
Arguments:
- jac: bfloat16 [16, 64, 3, 128, 128], P('tm', 'net'), may hold values from -0.5 to 1.5
- block_cols: int32 [64, 2], P('net'), may hold values from 0 to 3
- iface_jac: bfloat16 [16, 16, 16, 128, 128], P('tm', 'net'), may hold values from -0.1796875 to 0.1796875
- iface_send: int32 [16, 16], P('net'), may hold values from 0 to 3
- iface_recv: int32 [16, 16], P('net'), may hold values from 0 to 3
- iface_live: int32 [16, 16], P('net'), may hold values from 0 to 128
- ctrl_node: int32 [768], P('cols'), may hold values from 0 to 8191
- ctrl_gain: float32 [16, 768], P('tm', 'cols'), may hold values from -6 to 6
Outputs:
- sens: bfloat16 [16, 768, 8192], P('tm', 'cols', 'net')
All inputs are finite; a program needn't handle non-finite values.
Results may differ from a plain program's by a relative error of at most 0.013.
Values may be sent and summed in bfloat16 or wider, within the bound.
A program may use at most 64 MiB of HBM per device.

v0:
```python
import jax
import jax.numpy as jnp
from jax import lax
from jax.sharding import PartitionSpec as P


def from_behind(value, axis, by):
    size = lax.axis_size(axis)
    pairs = [(i, i + by) for i in range(size) if 0 <= i + by < size]
    return lax.ppermute(value, axis, pairs)


def local(jac, block_cols, iface_jac, iface_send, iface_recv, iface_live, ctrl_node, ctrl_gain):
    step_count = jac.shape[0]
    block_count = jac.shape[1]
    block_size = jac.shape[3]
    col_count = ctrl_node.shape[0]
    tm_size = lax.axis_size("tm")
    section_index = lax.axis_index("tm")
    partition = lax.axis_index("net")
    state_count = block_count * block_size
    global_rows = partition * state_count + jnp.arange(state_count, dtype=jnp.int32)
    receive_map = (
        iface_recv[0][:, None] == jnp.arange(block_count, dtype=jnp.int32)[None, :]
    ).astype(jnp.float32)
    live_mask = (jnp.arange(block_size, dtype=jnp.int32)[None, :] < iface_live[0][:, None]).astype(
        jnp.float32
    )
    send_rows = iface_send[0]
    highest = lax.Precision.HIGHEST

    def advance(state, step_jac, step_iface, node_ids, gain_row):
        width_cols = state.shape[0]
        state_tiles = state.reshape(width_cols, block_count, block_size)
        summed = jnp.einsum(
            "iab,cib->cia", step_jac[:, 0], state_tiles, preferred_element_type=jnp.float32
        )
        near_tiles = state_tiles[:, block_cols, :]
        summed = summed + jnp.einsum(
            "ikab,cikb->cia", step_jac[:, 1:], near_tiles, preferred_element_type=jnp.float32
        )
        outgoing = state_tiles[:, send_rows, :]
        incoming = lax.all_to_all(outgoing, "net", split_axis=1, concat_axis=1, tiled=True)
        coupled = jnp.einsum(
            "qab,cqb->cqa", step_iface, incoming, preferred_element_type=jnp.float32
        )
        coupled = coupled * live_mask[None]
        summed = summed + jnp.einsum("cqa,qi->cia", coupled, receive_map, precision=highest)
        injection = gain_row[:, None] * (node_ids[:, None] == global_rows[None, :]).astype(
            jnp.float32
        )
        return (summed.reshape(width_cols, state_count) + injection).astype(jnp.bfloat16)

    panel_count = 1
    panel_cols = col_count // panel_count

    def one_round(r, carry):
        results, finished = carry
        arrived = from_behind(finished, "tm", 1)
        lag_rounds = r - section_index
        panel_index = jnp.clip(lag_rounds, 0, panel_count - 1)
        first_col = panel_index * panel_cols
        state = arrived
        produced = []
        for s in range(step_count):
            gain_row = ctrl_gain[s]
            state = advance(state, jac[s], iface_jac[s, 0], ctrl_node, gain_row)
            produced.append(state)
        new_steps = jnp.stack(produced)
        written = lax.dynamic_update_slice_in_dim(results, new_steps, first_col, 1)
        in_range = jnp.logical_and(lag_rounds >= 0, lag_rounds < panel_count)
        results = jnp.where(in_range, written, results)
        return (results, state)

    results = jnp.zeros((step_count, col_count, state_count), jnp.bfloat16)
    finished = jnp.zeros((panel_cols, state_count), jnp.bfloat16)
    results, finished = lax.fori_loop(0, tm_size + panel_count - 1, one_round, (results, finished))
    return results


def solution(mesh):
    return jax.shard_map(
        local,
        mesh=mesh,
        in_specs=(
            P("tm", "net", None, None, None),
            P("net", None),
            P("tm", "net", None, None, None),
            P("net", None),
            P("net", None),
            P("net", None),
            P("cols"),
            P("tm", "cols"),
        ),
        out_specs=P("tm", "cols", "net"),
        check_vma=False,
    )
```

profile of v0, /device:TPU:12, one launch (start us, length us, event | category | flops | bytes accessed | tf_op | source)
XLA Modules:
  0.0 882.0 jit_solution(5332240637533575581)
XLA Ops:
  2.2 879.0 %while.16 = (s32[]{:T(128)}, bf16[2,192,512]{2,1,0:T(8,128)(2,1)S(1)}, bf16[192,512]{1,0:T(8,128)(2,1)S(1)}, s32[]{:T(128)}, bf16[2,4,3,128,128]{4,3,1,2,0:T(8,1...) while((s32[]{:T(128)}, ...), condition=%wide.region_1.2_spmd.clone, body=%wide.region_0.1_spmd.clone.sunk | while | flops 393420096 | bytes 33738568 | solution.py:77
  10.9 15.2 %all-to-all-start = ((bf16[192,16,128]{2,0,1:T(8,128)(2,1)}), bf16[192,16,128]{2,0,1:T(8,128)(2,1)S(1)}, u32[]{:S(2)}, u32[]{:S(2)}) async-start(bf16[192,16,128]{2,0,1:T(8,128)(2,1)} %bitcast.154), calls=%async_computation | async-start | bytes 1572864 | tf_op jit(solution)/shard_map/while/body/eval_jaxpr/all_to_all | solution.py:43
  28.4 36.0 %all-to-all-done = bf16[192,16,128]{2,0,1:T(8,128)(2,1)S(1)} async-done(((bf16[192,16,128]{2,0,1:T(8,128)(2,1)}), bf16[192,16,128]{2,0,1:T(8,128)(2,1)S(1)}, u32[]{:S(2)}, u32[]{:S(2)}) %all-to-all-start) | async-done | bytes 786464 | tf_op jit(solution)/shard_map/while/body/eval_jaxpr/all_to_all | solution.py:43
  69.6 7.7 all-to-all-start.1
  78.6 37.9 %all-to-all-done.1 = bf16[192,16,128]{2,0,1:T(8,128)(2,1)S(1)} async-done(((bf16[192,16,128]{2,0,1:T(8,128)(2,1)}), bf16[192,16,128]{2,0,1:T(8,128)(2,1)S(1)}, u32[]{:S(2)}, u32[]{:S(2)}) %all-to-all-start.1) | async-done | bytes 786464 | tf_op jit(solution)/shard_map/while/body/eval_jaxpr/all_to_all | solution.py:43
  129.5 7.5 all-to-all-start
  139.4 35.4 %all-to-all-done = bf16[192,16,128]{2,0,1:T(8,128)(2,1)S(1)} async-done(((bf16[192,16,128]{2,0,1:T(8,128)(2,1)}), bf16[192,16,128]{2,0,1:T(8,128)(2,1)S(1)}, u32[]{:S(2)}, u32[]{:S(2)}) %all-to-all-start) | async-done | bytes 786464 | tf_op jit(solution)/shard_map/while/body/eval_jaxpr/all_to_all | solution.py:43
  180.0 7.9 all-to-all-start.1
  189.2 37.9 %all-to-all-done.1 = bf16[192,16,128]{2,0,1:T(8,128)(2,1)S(1)} async-done(((bf16[192,16,128]{2,0,1:T(8,128)(2,1)}), bf16[192,16,128]{2,0,1:T(8,128)(2,1)S(1)}, u32[]{:S(2)}, u32[]{:S(2)}) %all-to-all-start.1) | async-done | bytes 786464 | tf_op jit(solution)/shard_map/while/body/eval_jaxpr/all_to_all | solution.py:43
  250.0 33.6 %all-to-all-done = bf16[192,16,128]{2,0,1:T(8,128)(2,1)S(1)} async-done(((bf16[192,16,128]{2,0,1:T(8,128)(2,1)}), bf16[192,16,128]{2,0,1:T(8,128)(2,1)S(1)}, u32[]{:S(2)}, u32[]{:S(2)}) %all-to-all-start) | async-done | bytes 786464 | tf_op jit(solution)/shard_map/while/body/eval_jaxpr/all_to_all | solution.py:43
  288.8 8.3 all-to-all-start.1
  298.5 36.8 %all-to-all-done.1 = bf16[192,16,128]{2,0,1:T(8,128)(2,1)S(1)} async-done(((bf16[192,16,128]{2,0,1:T(8,128)(2,1)}), bf16[192,16,128]{2,0,1:T(8,128)(2,1)S(1)}, u32[]{:S(2)}, u32[]{:S(2)}) %all-to-all-start.1) | async-done | bytes 786464 | tf_op jit(solution)/shard_map/while/body/eval_jaxpr/all_to_all | solution.py:43
  348.3 7.7 all-to-all-start
  358.4 33.4 %all-to-all-done = bf16[192,16,128]{2,0,1:T(8,128)(2,1)S(1)} async-done(((bf16[192,16,128]{2,0,1:T(8,128)(2,1)}), bf16[192,16,128]{2,0,1:T(8,128)(2,1)S(1)}, u32[]{:S(2)}, u32[]{:S(2)}) %all-to-all-start) | async-done | bytes 786464 | tf_op jit(solution)/shard_map/while/body/eval_jaxpr/all_to_all | solution.py:43
  397.0 8.4 all-to-all-start.1
  406.8 36.8 %all-to-all-done.1 = bf16[192,16,128]{2,0,1:T(8,128)(2,1)S(1)} async-done(((bf16[192,16,128]{2,0,1:T(8,128)(2,1)}), bf16[192,16,128]{2,0,1:T(8,128)(2,1)S(1)}, u32[]{:S(2)}, u32[]{:S(2)}) %all-to-all-start.1) | async-done | bytes 786464 | tf_op jit(solution)/shard_map/while/body/eval_jaxpr/all_to_all | solution.py:43
  456.6 7.7 all-to-all-start
  466.7 33.4 %all-to-all-done = bf16[192,16,128]{2,0,1:T(8,128)(2,1)S(1)} async-done(((bf16[192,16,128]{2,0,1:T(8,128)(2,1)}), bf16[192,16,128]{2,0,1:T(8,128)(2,1)S(1)}, u32[]{:S(2)}, u32[]{:S(2)}) %all-to-all-start) | async-done | bytes 786464 | tf_op jit(solution)/shard_map/while/body/eval_jaxpr/all_to_all | solution.py:43
  505.3 8.4 all-to-all-start.1
  515.1 36.8 %all-to-all-done.1 = bf16[192,16,128]{2,0,1:T(8,128)(2,1)S(1)} async-done(((bf16[192,16,128]{2,0,1:T(8,128)(2,1)}), bf16[192,16,128]{2,0,1:T(8,128)(2,1)S(1)}, u32[]{:S(2)}, u32[]{:S(2)}) %all-to-all-start.1) | async-done | bytes 786464 | tf_op jit(solution)/shard_map/while/body/eval_jaxpr/all_to_all | solution.py:43
  564.9 7.7 all-to-all-start
  575.0 33.4 %all-to-all-done = bf16[192,16,128]{2,0,1:T(8,128)(2,1)S(1)} async-done(((bf16[192,16,128]{2,0,1:T(8,128)(2,1)}), bf16[192,16,128]{2,0,1:T(8,128)(2,1)S(1)}, u32[]{:S(2)}, u32[]{:S(2)}) %all-to-all-start) | async-done | bytes 786464 | tf_op jit(solution)/shard_map/while/body/eval_jaxpr/all_to_all | solution.py:43
  613.6 8.4 all-to-all-start.1
  623.4 36.8 %all-to-all-done.1 = bf16[192,16,128]{2,0,1:T(8,128)(2,1)S(1)} async-done(((bf16[192,16,128]{2,0,1:T(8,128)(2,1)}), bf16[192,16,128]{2,0,1:T(8,128)(2,1)S(1)}, u32[]{:S(2)}, u32[]{:S(2)}) %all-to-all-start.1) | async-done | bytes 786464 | tf_op jit(solution)/shard_map/while/body/eval_jaxpr/all_to_all | solution.py:43
  673.2 7.7 all-to-all-start
  683.3 33.4 %all-to-all-done = bf16[192,16,128]{2,0,1:T(8,128)(2,1)S(1)} async-done(((bf16[192,16,128]{2,0,1:T(8,128)(2,1)}), bf16[192,16,128]{2,0,1:T(8,128)(2,1)S(1)}, u32[]{:S(2)}, u32[]{:S(2)}) %all-to-all-start) | async-done | bytes 786464 | tf_op jit(solution)/shard_map/while/body/eval_jaxpr/all_to_all | solution.py:43
  721.9 8.4 all-to-all-start.1
  731.7 36.8 %all-to-all-done.1 = bf16[192,16,128]{2,0,1:T(8,128)(2,1)S(1)} async-done(((bf16[192,16,128]{2,0,1:T(8,128)(2,1)}), bf16[192,16,128]{2,0,1:T(8,128)(2,1)S(1)}, u32[]{:S(2)}, u32[]{:S(2)}) %all-to-all-start.1) | async-done | bytes 786464 | tf_op jit(solution)/shard_map/while/body/eval_jaxpr/all_to_all | solution.py:43
  781.5 7.7 all-to-all-start
  791.6 33.4 %all-to-all-done = bf16[192,16,128]{2,0,1:T(8,128)(2,1)S(1)} async-done(((bf16[192,16,128]{2,0,1:T(8,128)(2,1)}), bf16[192,16,128]{2,0,1:T(8,128)(2,1)S(1)}, u32[]{:S(2)}, u32[]{:S(2)}) %all-to-all-start) | async-done | bytes 786464 | tf_op jit(solution)/shard_map/while/body/eval_jaxpr/all_to_all | solution.py:43
  830.2 8.4 all-to-all-start.1
  840.0 36.8 %all-to-all-done.1 = bf16[192,16,128]{2,0,1:T(8,128)(2,1)S(1)} async-done(((bf16[192,16,128]{2,0,1:T(8,128)(2,1)}), bf16[192,16,128]{2,0,1:T(8,128)(2,1)S(1)}, u32[]{:S(2)}, u32[]{:S(2)}) %all-to-all-start.1) | async-done | bytes 786464 | tf_op jit(solution)/shard_map/while/body/eval_jaxpr/all_to_all | solution.py:43
  (290 shorter events, 184.3 us)
Async XLA Ops:
  0.0 2.2 copy-start.6
  0.0 2.2 copy-start.5
  0.0 2.2 copy-start.2
  0.0 2.2 copy-start.4
  0.0 2.2 copy-start.1
  0.0 2.2 copy-start.3
  2.3 7.0 collective-permute-start
  10.9 53.5 %all-to-all-start = ((bf16[192,16,128]{2,0,1:T(8,128)(2,1)}), bf16[192,16,128]{2,0,1:T(8,128)(2,1)S(1)}, u32[]{:S(2)}, u32[]{:S(2)}) async-start(bf16[192,16,128]{2,0,1:T(8,128)(2,1)} %bitcast.154), calls=%async_computation | async-start | bytes 1572864 | tf_op jit(solution)/shard_map/while/body/eval_jaxpr/all_to_all | solution.py:43
  69.6 46.9 %all-to-all-start.1 = ((bf16[192,16,128]{2,0,1:T(8,128)(2,1)}), bf16[192,16,128]{2,0,1:T(8,128)(2,1)S(1)}, u32[]{:S(2)}, u32[]{:S(2)}) async-start(bf16[192,16,128]{2,0,1:T(8,128)(2,1)} %bitcast.157), calls=%async_computation.1 | async-start | bytes 1572864 | tf_op jit(solution)/shard_map/while/body/eval_jaxpr/all_to_all | solution.py:43
  121.0 7.0 collective-permute-start
  129.5 45.3 %all-to-all-start = ((bf16[192,16,128]{2,0,1:T(8,128)(2,1)}), bf16[192,16,128]{2,0,1:T(8,128)(2,1)S(1)}, u32[]{:S(2)}, u32[]{:S(2)}) async-start(bf16[192,16,128]{2,0,1:T(8,128)(2,1)} %bitcast.154), calls=%async_computation | async-start | bytes 1572864 | tf_op jit(solution)/shard_map/while/body/eval_jaxpr/all_to_all | solution.py:43
  180.0 47.1 %all-to-all-start.1 = ((bf16[192,16,128]{2,0,1:T(8,128)(2,1)}), bf16[192,16,128]{2,0,1:T(8,128)(2,1)S(1)}, u32[]{:S(2)}, u32[]{:S(2)}) async-start(bf16[192,16,128]{2,0,1:T(8,128)(2,1)} %bitcast.157), calls=%async_computation.1 | async-start | bytes 1572864 | tf_op jit(solution)/shard_map/while/body/eval_jaxpr/all_to_all | solution.py:43
  231.6 7.0 collective-permute-start
  240.2 43.4 %all-to-all-start = ((bf16[192,16,128]{2,0,1:T(8,128)(2,1)}), bf16[192,16,128]{2,0,1:T(8,128)(2,1)S(1)}, u32[]{:S(2)}, u32[]{:S(2)}) async-start(bf16[192,16,128]{2,0,1:T(8,128)(2,1)} %bitcast.154), calls=%async_computation | async-start | bytes 1572864 | tf_op jit(solution)/shard_map/while/body/eval_jaxpr/all_to_all | solution.py:43
  288.8 46.5 %all-to-all-start.1 = ((bf16[192,16,128]{2,0,1:T(8,128)(2,1)}), bf16[192,16,128]{2,0,1:T(8,128)(2,1)S(1)}, u32[]{:S(2)}, u32[]{:S(2)}) async-start(bf16[192,16,128]{2,0,1:T(8,128)(2,1)} %bitcast.157), calls=%async_computation.1 | async-start | bytes 1572864 | tf_op jit(solution)/shard_map/while/body/eval_jaxpr/all_to_all | solution.py:43
  339.7 7.0 collective-permute-start
  348.3 43.5 %all-to-all-start = ((bf16[192,16,128]{2,0,1:T(8,128)(2,1)}), bf16[192,16,128]{2,0,1:T(8,128)(2,1)S(1)}, u32[]{:S(2)}, u32[]{:S(2)}) async-start(bf16[192,16,128]{2,0,1:T(8,128)(2,1)} %bitcast.154), calls=%async_computation | async-start | bytes 1572864 | tf_op jit(solution)/shard_map/while/body/eval_jaxpr/all_to_all | solution.py:43
  397.0 46.5 %all-to-all-start.1 = ((bf16[192,16,128]{2,0,1:T(8,128)(2,1)}), bf16[192,16,128]{2,0,1:T(8,128)(2,1)S(1)}, u32[]{:S(2)}, u32[]{:S(2)}) async-start(bf16[192,16,128]{2,0,1:T(8,128)(2,1)} %bitcast.157), calls=%async_computation.1 | async-start | bytes 1572864 | tf_op jit(solution)/shard_map/while/body/eval_jaxpr/all_to_all | solution.py:43
  448.0 7.0 collective-permute-start
  456.6 43.5 %all-to-all-start = ((bf16[192,16,128]{2,0,1:T(8,128)(2,1)}), bf16[192,16,128]{2,0,1:T(8,128)(2,1)S(1)}, u32[]{:S(2)}, u32[]{:S(2)}) async-start(bf16[192,16,128]{2,0,1:T(8,128)(2,1)} %bitcast.154), calls=%async_computation | async-start | bytes 1572864 | tf_op jit(solution)/shard_map/while/body/eval_jaxpr/all_to_all | solution.py:43
  505.3 46.5 %all-to-all-start.1 = ((bf16[192,16,128]{2,0,1:T(8,128)(2,1)}), bf16[192,16,128]{2,0,1:T(8,128)(2,1)S(1)}, u32[]{:S(2)}, u32[]{:S(2)}) async-start(bf16[192,16,128]{2,0,1:T(8,128)(2,1)} %bitcast.157), calls=%async_computation.1 | async-start | bytes 1572864 | tf_op jit(solution)/shard_map/while/body/eval_jaxpr/all_to_all | solution.py:43
  556.3 7.0 collective-permute-start
  564.9 43.5 %all-to-all-start = ((bf16[192,16,128]{2,0,1:T(8,128)(2,1)}), bf16[192,16,128]{2,0,1:T(8,128)(2,1)S(1)}, u32[]{:S(2)}, u32[]{:S(2)}) async-start(bf16[192,16,128]{2,0,1:T(8,128)(2,1)} %bitcast.154), calls=%async_computation | async-start | bytes 1572864 | tf_op jit(solution)/shard_map/while/body/eval_jaxpr/all_to_all | solution.py:43
  613.6 46.5 %all-to-all-start.1 = ((bf16[192,16,128]{2,0,1:T(8,128)(2,1)}), bf16[192,16,128]{2,0,1:T(8,128)(2,1)S(1)}, u32[]{:S(2)}, u32[]{:S(2)}) async-start(bf16[192,16,128]{2,0,1:T(8,128)(2,1)} %bitcast.157), calls=%async_computation.1 | async-start | bytes 1572864 | tf_op jit(solution)/shard_map/while/body/eval_jaxpr/all_to_all | solution.py:43
  664.6 7.0 collective-permute-start
  673.2 43.5 %all-to-all-start = ((bf16[192,16,128]{2,0,1:T(8,128)(2,1)}), bf16[192,16,128]{2,0,1:T(8,128)(2,1)S(1)}, u32[]{:S(2)}, u32[]{:S(2)}) async-start(bf16[192,16,128]{2,0,1:T(8,128)(2,1)} %bitcast.154), calls=%async_computation | async-start | bytes 1572864 | tf_op jit(solution)/shard_map/while/body/eval_jaxpr/all_to_all | solution.py:43
  721.9 46.6 %all-to-all-start.1 = ((bf16[192,16,128]{2,0,1:T(8,128)(2,1)}), bf16[192,16,128]{2,0,1:T(8,128)(2,1)S(1)}, u32[]{:S(2)}, u32[]{:S(2)}) async-start(bf16[192,16,128]{2,0,1:T(8,128)(2,1)} %bitcast.157), calls=%async_computation.1 | async-start | bytes 1572864 | tf_op jit(solution)/shard_map/while/body/eval_jaxpr/all_to_all | solution.py:43
  772.9 7.0 collective-permute-start
  781.5 43.5 %all-to-all-start = ((bf16[192,16,128]{2,0,1:T(8,128)(2,1)}), bf16[192,16,128]{2,0,1:T(8,128)(2,1)S(1)}, u32[]{:S(2)}, u32[]{:S(2)}) async-start(bf16[192,16,128]{2,0,1:T(8,128)(2,1)} %bitcast.154), calls=%async_computation | async-start | bytes 1572864 | tf_op jit(solution)/shard_map/while/body/eval_jaxpr/all_to_all | solution.py:43
  830.2 46.5 %all-to-all-start.1 = ((bf16[192,16,128]{2,0,1:T(8,128)(2,1)}), bf16[192,16,128]{2,0,1:T(8,128)(2,1)S(1)}, u32[]{:S(2)}, u32[]{:S(2)}) async-start(bf16[192,16,128]{2,0,1:T(8,128)(2,1)} %bitcast.157), calls=%async_computation.1 | async-start | bytes 1572864 | tf_op jit(solution)/shard_map/while/body/eval_jaxpr/all_to_all | solution.py:43
  881.2 0.7 copy-start
where the time goes:
time: 885 us; the launch traced here: 882 us
  waiting for transfers between devices  609 us (69%)
  starting transfers between devices  150 us (17%)
  matrix products  60.9 us (7%)
  local copies, waits for them, and re-layouts  55.7 us (6%)
    all_to_all x16, waiting for transfers between devices, advance(): lax.all_to_all(outgoing, 'net', split_axis=1, concat_axis=1, tiled=True)  569 us
    all_to_all x16, starting transfers between devices, advance(): lax.all_to_all(outgoing, 'net', split_axis=1, concat_axis=1, tiled=True)  135 us
    ppermute x8, waiting for transfers between devices, from_behind(): return lax.ppermute(value, axis, pairs)  40.3 us
    dot_general x16, matrix products, advance(): jnp.einsum('cqa,qi->cia', coupled, receive_map, precision=highest)  29.1 us
    gather x16, local copies, waits for them, and re-layouts, advance(): outgoing = state_tiles[:, send_rows, :]  25.1 us
    dot_general x16, matrix products, advance(): jnp.einsum('qab,cqb->cqa', step_iface, incoming, preferred_element_type=j...  24.1 us
  transfers between devices with their start and end apart: 24, of which 24 were waited for; matrix products, arithmetic and copies ran while one was open for 3% of the time, Pallas kernels for 0%

commit v1 on v0

v1 whole, which is shorter than its diff:
```python
import jax
import jax.numpy as jnp
from jax import lax
from jax.experimental import pallas as pl
from jax.experimental.pallas import tpu as pltpu
from jax.sharding import PartitionSpec as P

MESH = pl.DeviceIdType.MESH
TM = 8
NET = 16
COLS = 4
NB = 4
BLK = 128
STEPS = 16
WIDE = 192
W = WIDE // TM
Q = NET // COLS
NEAR = sorted(range(1, NET), key=lambda d: min(d, NET - d))
FAR = NEAR[::-1]


def dot_t(x, w):
    return lax.dot_general(
        x, w, (((1,), (1,)), ((), ())), preferred_element_type=jnp.float32
    )


def kernel(
    jac, iface, bcols, send, recv, live, node, gain, out,
    ja, ia, gains, state, zero, wide, wide_out, stage, sbuf, rbuf,
    own_sem, quarter_sem, sib_sem, ysend, sibsend, xsend,
    gain_send, gain_recv, first_send, first_recv,
    ex_send, ex_recv, out_send, out_recv,
):
    tm = lax.axis_index("tm")
    me = lax.axis_index("net")
    x = lax.axis_index("cols")
    y, core = tm // 2, lax.rem(tm, 2)
    sibling = 2 * y + 1 - core
    lane = lax.broadcasted_iota(jnp.int32, (1, BLK), 1)

    def remote(src, dst, ssem, rsem, **device):
        return pltpu.make_async_remote_copy(
            src_ref=src, dst_ref=dst, send_sem=ssem, recv_sem=rsem,
            device_id=device, device_id_type=MESH,
        )

    def wait(ref, sem):
        pltpu.make_async_copy(ref, ref, sem).wait()

    barrier = pltpu.get_barrier_semaphore()
    for d in FAR:
        pl.semaphore_signal(barrier, inc=1, device_id={"net": lax.rem(me + d, NET)}, device_id_type=MESH)
    for d in range(1, TM):
        pl.semaphore_signal(barrier, inc=1, device_id={"tm": lax.rem(tm + d, TM)}, device_id_type=MESH)
    for d in range(1, COLS):
        pl.semaphore_signal(barrier, inc=1, device_id={"cols": lax.rem(x + d, COLS)}, device_id_type=MESH)

    own = []
    for s in range(2):
        own.append(pltpu.make_async_copy(jac.at[s], ja.at[2 * tm + s], own_sem.at[s, 0]))
        own.append(pltpu.make_async_copy(iface.at[s], ia.at[2 * tm + s], own_sem.at[s, 1]))
    for copy in own:
        copy.start()

    def near_terms(t, ref):
        sums = []
        for i in range(NB):
            values = jnp.concatenate([ref[i], ref[bcols[i, 0]], ref[bcols[i, 1]]], axis=1)
            weights = jnp.concatenate([ja[t, i, 0], ja[t, i, 1], ja[t, i, 2]], axis=1)
            sums.append(dot_t(values, weights))
        return sums

    def add_interface(sums, t, q, values):
        term = dot_t(values, ia[t, q])
        reach, block = live[0, q], recv[0, q]
        return [
            total + jnp.where(lane < jnp.where(block == i, reach, 0), term, 0.0)
            for i, total in enumerate(sums)
        ]

    def inject(total, i, nodes, gain_rows):
        return total + jnp.where(nodes == lane + (me * NB + i) * BLK, gain_rows, 0.0)

    for copy in own:
        copy.wait()
    gains[pl.ds(2 * tm, 2)] = gain[tm]

    @pl.when(tm == 0)
    def _():
        zero[...] = jnp.zeros_like(zero)
        sums = near_terms(0, zero)
        for q in range(NET):
            sums = add_interface(sums, 0, q, zero[0])
        for i in range(NB):
            for g in range(TM):
                rows = sums[i][g * W : (g + 1) * W]
                new = inject(rows, i, node[g], gain[g, 0]).astype(jnp.bfloat16)
                wide[g, i] = new
                wide_out[g, :, i * BLK : (i + 1) * BLK] = new
        pltpu.make_async_copy(wide_out, out.at[0], out_recv.at[0, 0]).start()
        state[...] = wide[0]

    pl.semaphore_wait(barrier, NET - 1 + TM - 1 + COLS - 1)

    @pl.when(tm == 0)
    def _():
        for g in range(1, TM):
            remote(wide.at[g], state, first_send.at[g], first_recv, tm=g).start()

    def j_part(t, k):
        return ja.at[t, k]

    def i_part(t, k):
        return ia.at[t, pl.ds(k * Q, Q)]

    def spread_own(s):
        t = 2 * tm + s
        for d in range(1, 4):
            there = 2 * lax.rem(y + d, 4) + core
            remote(jac.at[s, x], j_part(t, x), ysend.at[s, 0], quarter_sem.at[t, x, 0], tm=there).start()
            remote(iface.at[s, pl.ds(x * Q, Q)], i_part(t, x), ysend.at[s, 1], quarter_sem.at[t, x, 1], tm=there).start()
        remote(jac.at[s], ja.at[t], sibsend.at[t, 0], sib_sem.at[t, 0], tm=sibling).start()
        remote(iface.at[s], ia.at[t], sibsend.at[t, 1], sib_sem.at[t, 1], tm=sibling).start()

    def to_sibling(t, k):
        remote(j_part(t, k), j_part(t, k), sibsend.at[t, 0], sib_sem.at[t, 0], tm=sibling).start()
        remote(i_part(t, k), i_part(t, k), sibsend.at[t, 1], sib_sem.at[t, 1], tm=sibling).start()

    def forwards(t):
        return jnp.logical_and(
            t < STEPS, jnp.logical_and(lax.rem(t // 2, 2) == core, t // 4 != y)
        )

    def forward_own_quarter(t):
        @pl.when(forwards(t))
        def _():
            wait(j_part(t, x), quarter_sem.at[t, x, 0])
            wait(i_part(t, x), quarter_sem.at[t, x, 1])
            for d in range(1, COLS):
                there = lax.rem(x + d, COLS)
                remote(j_part(t, x), j_part(t, x), xsend.at[t, 0], quarter_sem.at[t, x, 0], cols=there).start()
                remote(i_part(t, x), i_part(t, x), xsend.at[t, 1], quarter_sem.at[t, x, 1], cols=there).start()
            to_sibling(t, x)

    def forward_other_quarters(t):
        @pl.when(forwards(t))
        def _():
            for d in range(1, COLS):
                k = lax.rem(x + d, COLS)
                wait(j_part(t, k), quarter_sem.at[t, k, 0])
                wait(i_part(t, k), quarter_sem.at[t, k, 1])
                to_sibling(t, k)

    def from_sibling(t):
        @pl.when(lax.rem(t // 2, 2) != core)
        def _():
            wait(ja.at[t], sib_sem.at[t, 0])
            wait(ia.at[t], sib_sem.at[t, 1])

    @pl.when(y == 0)
    def _():
        @pl.when(tm != 0)
        def _():
            spread_own(0)

        spread_own(1)

    for d in range(1, TM):
        there = lax.rem(tm + d, TM)
        remote(gain.at[there], gains.at[pl.ds(2 * tm, 2)], gain_send.at[d], gain_recv.at[d], tm=there).start()

    @pl.when(tm != 0)
    def _():
        wait(state, first_recv)

    def exchange(t):
        slot = lax.rem(t, 2)
        for d in FAR:
            p = lax.rem(me + d, NET)
            sbuf[slot, d] = state[send[0, p]]
            remote(sbuf.at[slot, d], rbuf.at[slot, d], ex_send.at[slot, d], ex_recv.at[slot, d], net=p).start()

    def step(t, carry):
        slot = lax.rem(t, 2)
        exchange(t)

        @pl.when(t == 1)
        def _():
            forward_own_quarter(1)
            forward_own_quarter(2)
            forward_other_quarters(1)

        @pl.when(jnp.logical_and(y > 0, t == jnp.maximum(4 * y - 4, 1)))
        def _():
            spread_own(0)
            spread_own(1)

        forward_own_quarter(t + 2)
        forward_other_quarters(t + 1)
        from_sibling(t)

        @pl.when(t == 1)
        def _():
            for d in range(1, TM):
                source = lax.rem(tm - d + TM, TM)
                wait(gains.at[pl.ds(2 * source, 2)], gain_recv.at[d])

        sums = near_terms(t, state)
        sums = add_interface(sums, t, me, state[send[0, me]])
        for d in NEAR:
            wait(rbuf.at[slot, d], ex_recv.at[slot, d])
            sums = add_interface(sums, t, lax.rem(me - d + NET, NET), rbuf[slot, d])
        nodes, gain_rows = node[tm], gains[t]
        for i in range(NB):
            new = inject(sums[i], i, nodes, gain_rows).astype(jnp.bfloat16)
            state[i] = new
            stage[t, :, i * BLK : (i + 1) * BLK] = new

        there, s = t // 2, lax.rem(t, 2)

        @pl.when(there == tm)
        def _():
            pltpu.make_async_copy(stage.at[t], out.at[s, tm], out_recv.at[s, tm]).start()

        @pl.when(there != tm)
        def _():
            remote(stage.at[t], out.at[s, tm], out_send.at[t], out_recv.at[s, tm], tm=there).start()

        for d in FAR:
            wait(sbuf.at[slot, d], ex_send.at[slot, d])
        return carry

    lax.fori_loop(1, STEPS, step, 0)

    def drain(t, carry):
        @pl.when(forwards(t))
        def _():
            wait(ja.at[t, pl.ds(0, 3)], xsend.at[t, 0])
            wait(ia.at[t, pl.ds(0, 3 * Q)], xsend.at[t, 1])

        @pl.when(lax.rem(t // 2, 2) == core)
        def _():
            wait(ja.at[t], sibsend.at[t, 0])
            wait(ia.at[t], sibsend.at[t, 1])

        @pl.when(t // 2 != tm)
        def _():
            wait(stage.at[t], out_send.at[t])

        return carry

    lax.fori_loop(1, STEPS, drain, 0)
    for s in range(2):
        @pl.when(jnp.logical_or(tm != 0, s == 1))
        def _(s=s):
            wait(ja.at[0, pl.ds(0, 3)], ysend.at[s, 0])
            wait(ia.at[0, pl.ds(0, 3 * Q)], ysend.at[s, 1])
            for g in range(TM):
                wait(stage.at[0], out_recv.at[s, g])

    for d in range(1, TM):
        wait(gain.at[0], gain_send.at[d])

    @pl.when(tm == 0)
    def _():
        pltpu.make_async_copy(wide_out, out.at[0], out_recv.at[0, 0]).wait()
        for g in range(1, TM):
            wait(state, first_send.at[g])


def local(jac, block_cols, iface_jac, iface_send, iface_recv, iface_live, ctrl_node, ctrl_gain):
    node = jnp.broadcast_to(ctrl_node.reshape(TM, W, 1), (TM, W, BLK))
    gain = jnp.broadcast_to(
        ctrl_gain.reshape(2, TM, W, 1).transpose(1, 0, 2, 3), (TM, 2, W, BLK)
    )
    smem = pl.BlockSpec(memory_space=pltpu.SMEM)
    vmem = pl.BlockSpec(memory_space=pltpu.VMEM)
    hbm = pl.BlockSpec(memory_space=pl.ANY)
    dma = pltpu.SemaphoreType.DMA
    bf16, f32 = jnp.bfloat16, jnp.float32
    out = pl.pallas_call(
        kernel,
        out_shape=jax.ShapeDtypeStruct((2, TM, W, NB * BLK), bf16),
        in_specs=[hbm, hbm, smem, smem, smem, smem, vmem, vmem],
        out_specs=hbm,
        scratch_shapes=[
            pltpu.VMEM((STEPS, NB, 3, BLK, BLK), bf16),
            pltpu.VMEM((STEPS, NET, BLK, BLK), bf16),
            pltpu.VMEM((STEPS, W, BLK), f32),
            pltpu.VMEM((NB, W, BLK), bf16),
            pltpu.VMEM((NB, WIDE, BLK), bf16),
            pltpu.VMEM((TM, NB, W, BLK), bf16),
            pltpu.VMEM((TM, W, NB * BLK), bf16),
            pltpu.VMEM((STEPS, W, NB * BLK), bf16),
            pltpu.VMEM((2, NET, W, BLK), bf16),
            pltpu.VMEM((2, NET, W, BLK), bf16),
            dma((2, 2)),
            dma((STEPS, COLS, 2)),
            dma((STEPS, 2)),
            dma((2, 2)),
            dma((STEPS, 2)),
            dma((STEPS, 2)),
            dma((TM,)),
            dma((TM,)),
            dma((TM,)),
            dma,
            dma((2, NET)),
            dma((2, NET)),
            dma((STEPS,)),
            dma((2, TM)),
        ],
        compiler_params=pltpu.CompilerParams(
            collective_id=0, has_side_effects=True, vmem_limit_bytes=40 << 20
        ),
    )(
        jac, iface_jac.reshape(2, NET, BLK, BLK),
        block_cols, iface_send, iface_recv, iface_live, node, gain,
    )
    return out.reshape(2, WIDE, NB * BLK)


def solution(mesh):
    return jax.shard_map(
        local,
        mesh=mesh,
        in_specs=(
            P("tm", "net", None, None, None),
            P("net", None),
            P("tm", "net", None, None, None),
            P("net", None),
            P("net", None),
            P("net", None),
            P("cols"),
            P("tm", "cols"),
        ),
        out_specs=P("tm", "cols", "net"),
        check_vma=False,
    )
```

time: 885 us -> 173 us (0.20)
  the two profiles are of different devices: /device:TPU:12 before, /device:TPU:25 now
where the time goes in v1:
time: 173 us
  Pallas kernels  167 us (97%)
  local copies, waits for them, and re-layouts  5.97 us (3%)
    pallas_call x1, Pallas kernels, local(): pl.pallas_call(kernel, out_shape=jax.ShapeDtypeStruct((2, TM, W, NB * BLK...  167 us
    unnamed x18, local copies, waits for them, and re-layouts  5.62 us

profile of v1, /device:TPU:25, one launch (start us, length us, event | category | flops | bytes accessed | tf_op | source)
XLA Modules:
  0.0 173.2 jit_solution(7845036105117141990)
XLA Ops:
  0.0 0.0 copy-start.6
  0.0 0.7 copy-done.6
  0.7 0.0 copy-start.7
  0.7 0.1 copy.10.bcols
  0.8 0.6 copy-done.7
  1.4 0.0 copy-start.5
  1.4 0.1 broadcast_in_dim.14
  1.4 0.6 copy-done.5
  2.0 0.1 reshape.12
  2.1 0.1 broadcast_in_dim.15.node
  2.2 0.0 copy-start.2
  2.2 0.0 copy-start.3
  2.2 0.0 copy-start.4
  2.3 0.1 broadcast_in_dim.17.gain
  2.4 0.5 copy-done.2
  2.9 0.0 copy-done.3
  2.9 0.0 copy-done.4
  2.9 0.0 copy-start
  2.9 1.2 copy-done
  4.1 0.0 copy-start.1
  4.1 1.1 copy-done.1
  5.3 167.2 %shard_map.82 = bf16[2,8,24,512]{3,2,1,0:T(8,128)(2,1)S(1)} custom-call(bf16[2,4,3,128,128]{4,3,2,1,0:T(8,128)(2,1)S(1)} %copy-done.1, bf16[2,16,128,128]{3,2,1,0:T(8,128)(2,1)S(1)} %bitcast.8, s32[4,2]{1,0:T(4,128)S(1)} %copy.10.bcols, s32[1,16]{1,0:T(1,128)S(1)} %copy-done.2, s32[1,16]{1,0:T(1,128)S(1)} %copy-done.3, s32[1,16]{1,0:T(1,128)S(1)} %copy-done.4, ...), custom_call_target="tpu_custom_call" | custom-call | tf_op jit(solution)/shard_map/pallas_call | solution.py:282
  172.5 0.7 copy.14
  (1 shorter events, 0.0 us)
Async XLA Ops:
  0.0 0.7 copy-start.6
  0.7 0.7 copy-start.7
  1.4 0.7 copy-start.5
  2.2 0.7 copy-start.2
  2.2 0.7 copy-start.3
  2.2 0.7 copy-start.4
  2.9 1.2 copy-start
  4.1 1.1 copy-start.1

commit v2 on v1

--- a/solution.py
+++ b/solution.py
@@ -17,6 +17,7 @@
 Q = NET // COLS
 NEAR = sorted(range(1, NET), key=lambda d: min(d, NET - d))
 FAR = NEAR[::-1]
+GROUPS = (NEAR[:8], NEAR[8:])
 
 
 def dot_t(x, w):
@@ -26,9 +27,9 @@
 
 
 def kernel(
-    jac, iface, bcols, send, recv, live, node, gain, out,
-    ja, ia, gains, state, zero, wide, wide_out, stage, sbuf, rbuf,
-    own_sem, quarter_sem, sib_sem, ysend, sibsend, xsend,
+    jac, iface, bcols_hbm, send_hbm, recv_hbm, live_hbm, node_hbm, gain_hbm, out,
+    ja, ia, bcols, send, recv, live, node_row, gains, state, zero, wide, wide_out, stage, sbuf, rbuf,
+    small_sem, own_sem, quarter_sem, sib_sem, ysend, sibsend, xsend,
     gain_send, gain_recv, first_send, first_recv,
     ex_send, ex_recv, out_send, out_recv,
 ):
@@ -56,17 +57,23 @@
     for d in range(1, COLS):
         pl.semaphore_signal(barrier, inc=1, device_id={"cols": lax.rem(x + d, COLS)}, device_id_type=MESH)
 
-    own = []
+    own = [
+        pltpu.make_async_copy(src, dst, small_sem.at[n])
+        for n, (src, dst) in enumerate((
+            (bcols_hbm, bcols), (send_hbm, send), (recv_hbm, recv), (live_hbm, live),
+            (node_hbm, node_row), (gain_hbm, gains.at[tm]),
+        ))
+    ]
     for s in range(2):
         own.append(pltpu.make_async_copy(jac.at[s], ja.at[2 * tm + s], own_sem.at[s, 0]))
-        own.append(pltpu.make_async_copy(iface.at[s], ia.at[2 * tm + s], own_sem.at[s, 1]))
+        own.append(pltpu.make_async_copy(iface.at[s, 0], ia.at[2 * tm + s], own_sem.at[s, 1]))
     for copy in own:
         copy.start()
 
     def near_terms(t, ref):
         sums = []
         for i in range(NB):
-            values = jnp.concatenate([ref[i], ref[bcols[i, 0]], ref[bcols[i, 1]]], axis=1)
+            values = jnp.concatenate([ref[i], ref[bcols[0, i]], ref[bcols[1, i]]], axis=1)
             weights = jnp.concatenate([ja[t, i, 0], ja[t, i, 1], ja[t, i, 2]], axis=1)
             sums.append(dot_t(values, weights))
         return sums
@@ -79,12 +86,21 @@
             for i, total in enumerate(sums)
         ]
 
+    wide_lane = lax.broadcasted_iota(jnp.int32, (W, WIDE), 1)
+    wide_row = lax.broadcasted_iota(jnp.int32, (W, WIDE), 0)
+
+    def column(row, g):
+        picked = jnp.where(wide_lane == wide_row + g * W, row, jnp.zeros_like(row))
+        return jnp.broadcast_to(jnp.sum(picked, axis=1, keepdims=True), (W, BLK))
+
+    def nodes_of(g):
+        return column(node_row[...].reshape(1, WIDE).astype(jnp.float32), g).astype(jnp.int32)
+
     def inject(total, i, nodes, gain_rows):
         return total + jnp.where(nodes == lane + (me * NB + i) * BLK, gain_rows, 0.0)
 
     for copy in own:
         copy.wait()
-    gains[pl.ds(2 * tm, 2)] = gain[tm]
 
     @pl.when(tm == 0)
     def _():
@@ -92,10 +108,10 @@
         sums = near_terms(0, zero)
         for q in range(NET):
             sums = add_interface(sums, 0, q, zero[0])
-        for i in range(NB):
-            for g in range(TM):
-                rows = sums[i][g * W : (g + 1) * W]
-                new = inject(rows, i, node[g], gain[g, 0]).astype(jnp.bfloat16)
+        for g in range(TM):
+            nodes, gain_rows = nodes_of(g), column(gains[0, 0:1], g)
+            for i in range(NB):
+                new = inject(sums[i], i, nodes, gain_rows).astype(jnp.bfloat16)
                 wide[g, i] = new
                 wide_out[g, :, i * BLK : (i + 1) * BLK] = new
         pltpu.make_async_copy(wide_out, out.at[0], out_recv.at[0, 0]).start()
@@ -114,14 +130,14 @@
     def i_part(t, k):
         return ia.at[t, pl.ds(k * Q, Q)]
 
-    def spread_own(s):
-        t = 2 * tm + s
+    def spread_own(t):
+        s = lax.rem(t, 2)
         for d in range(1, 4):
             there = 2 * lax.rem(y + d, 4) + core
             remote(jac.at[s, x], j_part(t, x), ysend.at[s, 0], quarter_sem.at[t, x, 0], tm=there).start()
-            remote(iface.at[s, pl.ds(x * Q, Q)], i_part(t, x), ysend.at[s, 1], quarter_sem.at[t, x, 1], tm=there).start()
+            remote(iface.at[s, 0, pl.ds(x * Q, Q)], i_part(t, x), ysend.at[s, 1], quarter_sem.at[t, x, 1], tm=there).start()
         remote(jac.at[s], ja.at[t], sibsend.at[t, 0], sib_sem.at[t, 0], tm=sibling).start()
-        remote(iface.at[s], ia.at[t], sibsend.at[t, 1], sib_sem.at[t, 1], tm=sibling).start()
+        remote(iface.at[s, 0], ia.at[t], sibsend.at[t, 1], sib_sem.at[t, 1], tm=sibling).start()
 
     def to_sibling(t, k):
         remote(j_part(t, k), j_part(t, k), sibsend.at[t, 0], sib_sem.at[t, 0], tm=sibling).start()
@@ -158,21 +174,23 @@
             wait(ja.at[t], sib_sem.at[t, 0])
             wait(ia.at[t], sib_sem.at[t, 1])
 
-    @pl.when(y == 0)
-    def _():
-        @pl.when(tm != 0)
-        def _():
-            spread_own(0)
-
-        spread_own(1)
+    def spread(t):
+        @pl.when(jnp.logical_and(t < STEPS, t // 2 == tm))
+        def _():
+            spread_own(t)
+
+    spread(1)
 
     for d in range(1, TM):
         there = lax.rem(tm + d, TM)
-        remote(gain.at[there], gains.at[pl.ds(2 * tm, 2)], gain_send.at[d], gain_recv.at[d], tm=there).start()
+        remote(gain_hbm, gains.at[tm], gain_send.at[d], gain_recv.at[d], tm=there).start()
 
     @pl.when(tm != 0)
     def _():
         wait(state, first_recv)
+
+    spread(2)
+    spread(3)
 
     def exchange(t):
         slot = lax.rem(t, 2)
@@ -181,57 +199,78 @@
             sbuf[slot, d] = state[send[0, p]]
             remote(sbuf.at[slot, d], rbuf.at[slot, d], ex_send.at[slot, d], ex_recv.at[slot, d], net=p).start()
 
+    def output(t):
+        there, s = t // 2, lax.rem(t, 2)
+
+        @pl.when(there == tm)
+        def _():
+            pltpu.make_async_copy(stage.at[t], out.at[s, tm], out_recv.at[s, tm]).start()
+
+        @pl.when(there != tm)
+        def _():
+            remote(stage.at[t], out.at[s, tm], out_send.at[t], out_recv.at[s, tm], tm=there).start()
+
+    def sent(slot):
+        for d in FAR:
+            wait(sbuf.at[slot, d], ex_send.at[slot, d])
+
+    nodes = nodes_of(tm)
+
     def step(t, carry):
         slot = lax.rem(t, 2)
         exchange(t)
 
+        @pl.when(t > 1)
+        def _():
+            output(t - 1)
+            sent(1 - slot)
+
+        spread(t + 3)
+
         @pl.when(t == 1)
         def _():
             forward_own_quarter(1)
+            forward_other_quarters(1)
             forward_own_quarter(2)
-            forward_other_quarters(1)
-
-        @pl.when(jnp.logical_and(y > 0, t == jnp.maximum(4 * y - 4, 1)))
-        def _():
-            spread_own(0)
-            spread_own(1)
-
-        forward_own_quarter(t + 2)
-        forward_other_quarters(t + 1)
+            for d in range(1, TM):
+                wait(gains.at[lax.rem(tm - d + TM, TM)], gain_recv.at[d])
+
+        @pl.when(t == 2)
+        def _():
+            forward_other_quarters(2)
+            forward_own_quarter(3)
+
+        @pl.when(t == 3)
+        def _():
+            forward_other_quarters(3)
+
+        @pl.when(t >= 2)
+        def _():
+            forward_own_quarter(t + 2)
+
+        @pl.when(t >= 3)
+        def _():
+            forward_other_quarters(t + 1)
+
         from_sibling(t)
 
-        @pl.when(t == 1)
-        def _():
-            for d in range(1, TM):
-                source = lax.rem(tm - d + TM, TM)
-                wait(gains.at[pl.ds(2 * source, 2)], gain_recv.at[d])
-
-        sums = near_terms(t, state)
+        gain_rows = column(gains[t // 2, pl.ds(lax.rem(t, 2), 1)], tm)
+        sums = [inject(total, i, nodes, gain_rows) for i, total in enumerate(near_terms(t, state))]
         sums = add_interface(sums, t, me, state[send[0, me]])
-        for d in NEAR:
-            wait(rbuf.at[slot, d], ex_recv.at[slot, d])
-            sums = add_interface(sums, t, lax.rem(me - d + NET, NET), rbuf[slot, d])
-        nodes, gain_rows = node[tm], gains[t]
+        for group in GROUPS:
+            for d in group:
+                wait(rbuf.at[slot, d], ex_recv.at[slot, d])
+            for d in group:
+                sums = add_interface(sums, t, lax.rem(me - d + NET, NET), rbuf[slot, d])
         for i in range(NB):
-            new = inject(sums[i], i, nodes, gain_rows).astype(jnp.bfloat16)
+            new = sums[i].astype(jnp.bfloat16)
             state[i] = new
             stage[t, :, i * BLK : (i + 1) * BLK] = new
-
-        there, s = t // 2, lax.rem(t, 2)
-
-        @pl.when(there == tm)
-        def _():
-            pltpu.make_async_copy(stage.at[t], out.at[s, tm], out_recv.at[s, tm]).start()
-
-        @pl.when(there != tm)
-        def _():
-            remote(stage.at[t], out.at[s, tm], out_send.at[t], out_recv.at[s, tm], tm=there).start()
-
-        for d in FAR:
-            wait(sbuf.at[slot, d], ex_send.at[slot, d])
         return carry
 
     lax.fori_loop(1, STEPS, step, 0)
+    output(STEPS - 1)
+    sent((STEPS - 1) % 2)
 
     def drain(t, carry):
         @pl.when(forwards(t))
@@ -260,7 +299,7 @@
                 wait(stage.at[0], out_recv.at[s, g])
 
     for d in range(1, TM):
-        wait(gain.at[0], gain_send.at[d])
+        wait(gains.at[0], gain_send.at[d])
 
     @pl.when(tm == 0)
     def _():
@@ -270,31 +309,31 @@
 
 
 def local(jac, block_cols, iface_jac, iface_send, iface_recv, iface_live, ctrl_node, ctrl_gain):
-    node = jnp.broadcast_to(ctrl_node.reshape(TM, W, 1), (TM, W, BLK))
-    gain = jnp.broadcast_to(
-        ctrl_gain.reshape(2, TM, W, 1).transpose(1, 0, 2, 3), (TM, 2, W, BLK)
-    )
-    smem = pl.BlockSpec(memory_space=pltpu.SMEM)
-    vmem = pl.BlockSpec(memory_space=pltpu.VMEM)
-    hbm = pl.BlockSpec(memory_space=pl.ANY)
+    hbm = pl.BlockSpec(memory_space=pltpu.HBM)
     dma = pltpu.SemaphoreType.DMA
-    bf16, f32 = jnp.bfloat16, jnp.float32
+    bf16, f32, i32 = jnp.bfloat16, jnp.float32, jnp.int32
     out = pl.pallas_call(
         kernel,
         out_shape=jax.ShapeDtypeStruct((2, TM, W, NB * BLK), bf16),
-        in_specs=[hbm, hbm, smem, smem, smem, smem, vmem, vmem],
+        in_specs=[hbm] * 8,
         out_specs=hbm,
         scratch_shapes=[
             pltpu.VMEM((STEPS, NB, 3, BLK, BLK), bf16),
             pltpu.VMEM((STEPS, NET, BLK, BLK), bf16),
-            pltpu.VMEM((STEPS, W, BLK), f32),
+            pltpu.SMEM((2, NB), i32),
+            pltpu.SMEM((1, NET), i32),
+            pltpu.SMEM((1, NET), i32),
+            pltpu.SMEM((1, NET), i32),
+            pltpu.VMEM((WIDE,), i32),
+            pltpu.VMEM((TM, 2, WIDE), f32),
             pltpu.VMEM((NB, W, BLK), bf16),
-            pltpu.VMEM((NB, WIDE, BLK), bf16),
+            pltpu.VMEM((NB, W, BLK), bf16),
             pltpu.VMEM((TM, NB, W, BLK), bf16),
             pltpu.VMEM((TM, W, NB * BLK), bf16),
             pltpu.VMEM((STEPS, W, NB * BLK), bf16),
             pltpu.VMEM((2, NET, W, BLK), bf16),
             pltpu.VMEM((2, NET, W, BLK), bf16),
+            dma((6,)),
             dma((2, 2)),
             dma((STEPS, COLS, 2)),
             dma((STEPS, 2)),
@@ -311,11 +350,10 @@
             dma((2, TM)),
         ],
         compiler_params=pltpu.CompilerParams(
-            collective_id=0, has_side_effects=True, vmem_limit_bytes=40 << 20
+            collective_id=0, has_side_effects=True, vmem_limit_bytes=60 << 20
         ),
     )(
-        jac, iface_jac.reshape(2, NET, BLK, BLK),
-        block_cols, iface_send, iface_recv, iface_live, node, gain,
+        jac, iface_jac, block_cols.T, iface_send, iface_recv, iface_live, ctrl_node, ctrl_gain
     )
     return out.reshape(2, WIDE, NB * BLK)
 

time: 173 us -> 160 us (0.925)
  Pallas kernels: 167 us -> 158 us
  local copies, waits for them, and re-layouts: 5.97 us -> 1.77 us
    pallas_call x1, Pallas kernels: 167 us -> 158 us  [local(): pl.pallas_call(kernel, out_shape=jax.ShapeDtypeStruct((2, TM, W, NB * BLK...]
    unnamed x18 -> x1, local copies, waits for them, and re-layouts: 5.62 us -> 1.77 us
where the time goes in v2:
time: 160 us
  Pallas kernels  158 us (99%)
  local copies, waits for them, and re-layouts  1.77 us (1%)
    pallas_call x1, Pallas kernels, local(): pl.pallas_call(kernel, out_shape=jax.ShapeDtypeStruct((2, TM, W, NB * BLK...  158 us

profile of v2, /device:TPU:25, one launch (start us, length us, event | category | flops | bytes accessed | tf_op | source)
XLA Modules:
  0.0 160.1 jit_solution(8107584409238841730)
XLA Ops:
  0.0 158.3 %shard_map.82 = bf16[2,8,24,512]{3,2,1,0:T(8,128)(2,1)} custom-call(bf16[2,4,3,128,128]{4,3,2,1,0:T(8,128)(2,1)} %jac.1, bf16[2,1,16,128,128]{4,3,2,1,0:T(8,128)(2,1)} %iface.1, s32[2,4]{1,0:T(2,128)} %bitcast.3, s32[1,16]{1,0:T(1,128)} %send_hbm.1, s32[1,16]{1,0:T(1,128)} %recv_hbm.1, s32[1,16]{1,0:T(1,128)} %live_hbm.1, s32[192]{0:T(256)} %node_hbm.1, ...), custom_call_target="tpu_custom_call" | custom-call | tf_op jit(solution)/shard_map/pallas_call | solution.py:315
  158.3 1.8 %copy.10 = bf16[2,192,512]{2,1,0:T(8,128)(2,1)} copy(bf16[2,192,512]{2,1,0:T(8,128)(2,1)} %bitcast.2) | data formatting | bytes 786432

commit v3 on v2

--- a/solution.py
+++ b/solution.py
@@ -124,55 +124,59 @@
         for g in range(1, TM):
             remote(wide.at[g], state, first_send.at[g], first_recv, tm=g).start()
 
-    def j_part(t, k):
-        return ja.at[t, k]
-
-    def i_part(t, k):
-        return ia.at[t, pl.ds(k * Q, Q)]
+    def part(t, k, kind):
+        return ja.at[t, k] if kind == 0 else ia.at[t, pl.ds(k * Q, Q)]
+
+    def whole(t, kind):
+        return ja.at[t] if kind == 0 else ia.at[t]
+
+    def three_parts(kind):
+        return ja.at[0, pl.ds(0, 3)] if kind == 0 else ia.at[0, pl.ds(0, 3 * Q)]
 
     def spread_own(t):
         s = lax.rem(t, 2)
-        for d in range(1, 4):
-            there = 2 * lax.rem(y + d, 4) + core
-            remote(jac.at[s, x], j_part(t, x), ysend.at[s, 0], quarter_sem.at[t, x, 0], tm=there).start()
-            remote(iface.at[s, 0, pl.ds(x * Q, Q)], i_part(t, x), ysend.at[s, 1], quarter_sem.at[t, x, 1], tm=there).start()
+        for d in (1, 3, 2):
+            row = lax.rem(y + d, 4)
+            remote(jac.at[s, x], part(t, x, 0), ysend.at[s, 0], quarter_sem.at[t, x], tm=2 * row).start()
+            remote(iface.at[s, 0, pl.ds(x * Q, Q)], part(t, x, 1), ysend.at[s, 1], quarter_sem.at[t, x], tm=2 * row + 1).start()
         remote(jac.at[s], ja.at[t], sibsend.at[t, 0], sib_sem.at[t, 0], tm=sibling).start()
         remote(iface.at[s, 0], ia.at[t], sibsend.at[t, 1], sib_sem.at[t, 1], tm=sibling).start()
 
-    def to_sibling(t, k):
-        remote(j_part(t, k), j_part(t, k), sibsend.at[t, 0], sib_sem.at[t, 0], tm=sibling).start()
-        remote(i_part(t, k), i_part(t, k), sibsend.at[t, 1], sib_sem.at[t, 1], tm=sibling).start()
-
-    def forwards(t):
-        return jnp.logical_and(
-            t < STEPS, jnp.logical_and(lax.rem(t // 2, 2) == core, t // 4 != y)
-        )
+    def forwarding(t, act):
+        for kind in range(2):
+            @pl.when(jnp.logical_and(jnp.logical_and(t < STEPS, t // 4 != y), core == kind))
+            def _(kind=kind):
+                act(kind)
+
+    def to_sibling(t, k, kind):
+        remote(part(t, k, kind), part(t, k, kind), sibsend.at[t, kind], sib_sem.at[t, kind], tm=sibling).start()
 
     def forward_own_quarter(t):
-        @pl.when(forwards(t))
-        def _():
-            wait(j_part(t, x), quarter_sem.at[t, x, 0])
-            wait(i_part(t, x), quarter_sem.at[t, x, 1])
-            for d in range(1, COLS):
-                there = lax.rem(x + d, COLS)
-                remote(j_part(t, x), j_part(t, x), xsend.at[t, 0], quarter_sem.at[t, x, 0], cols=there).start()
-                remote(i_part(t, x), i_part(t, x), xsend.at[t, 1], quarter_sem.at[t, x, 1], cols=there).start()
-            to_sibling(t, x)
+        def act(kind):
+            wait(part(t, x, kind), quarter_sem.at[t, x])
+            for d in (1, 3, 2):
+                remote(part(t, x, kind), part(t, x, kind), xsend.at[t], quarter_sem.at[t, x], cols=lax.rem(x + d, COLS)).start()
+            to_sibling(t, x, kind)
+
+        forwarding(t, act)
 
     def forward_other_quarters(t):
-        @pl.when(forwards(t))
-        def _():
-            for d in range(1, COLS):
+        def act(kind):
+            for d in (1, 3, 2):
                 k = lax.rem(x + d, COLS)
-                wait(j_part(t, k), quarter_sem.at[t, k, 0])
-                wait(i_part(t, k), quarter_sem.at[t, k, 1])
-                to_sibling(t, k)
+                wait(part(t, k, kind), quarter_sem.at[t, k])
+                to_sibling(t, k, kind)
+
+        forwarding(t, act)
 
     def from_sibling(t):
-        @pl.when(lax.rem(t // 2, 2) != core)
-        def _():
-            wait(ja.at[t], sib_sem.at[t, 0])
-            wait(ia.at[t], sib_sem.at[t, 1])
+        for kind in range(2):
+            here = jnp.logical_and(t // 4 != y, core != kind)
+            here = jnp.logical_or(here, jnp.logical_and(t // 4 == y, t // 2 != tm))
+
+            @pl.when(here)
+            def _(kind=kind):
+                wait(whole(t, kind), sib_sem.at[t, kind])
 
     def spread(t):
         @pl.when(jnp.logical_and(t < STEPS, t // 2 == tm))
@@ -188,9 +192,6 @@
     @pl.when(tm != 0)
     def _():
         wait(state, first_recv)
-
-    spread(2)
-    spread(3)
 
     def exchange(t):
         slot = lax.rem(t, 2)
@@ -225,10 +226,9 @@
             output(t - 1)
             sent(1 - slot)
 
-        spread(t + 3)
-
         @pl.when(t == 1)
         def _():
+            spread(2)
             forward_own_quarter(1)
             forward_other_quarters(1)
             forward_own_quarter(2)
@@ -246,6 +246,7 @@
 
         @pl.when(t >= 2)
         def _():
+            spread(t + 3)
             forward_own_quarter(t + 2)
 
         @pl.when(t >= 3)
@@ -253,6 +254,11 @@
             forward_other_quarters(t + 1)
 
         from_sibling(t)
+
+        @pl.when(t == 1)
+        def _():
+            spread(3)
+            spread(4)
 
         gain_rows = column(gains[t // 2, pl.ds(lax.rem(t, 2), 1)], tm)
         sums = [inject(total, i, nodes, gain_rows) for i, total in enumerate(near_terms(t, state))]
@@ -273,15 +279,17 @@
     sent((STEPS - 1) % 2)
 
     def drain(t, carry):
-        @pl.when(forwards(t))
-        def _():
-            wait(ja.at[t, pl.ds(0, 3)], xsend.at[t, 0])
-            wait(ia.at[t, pl.ds(0, 3 * Q)], xsend.at[t, 1])
-
-        @pl.when(lax.rem(t // 2, 2) == core)
-        def _():
-            wait(ja.at[t], sibsend.at[t, 0])
-            wait(ia.at[t], sibsend.at[t, 1])
+        def act(kind):
+            wait(three_parts(kind), xsend.at[t])
+            wait(whole(t, kind), sibsend.at[t, kind])
+
+        forwarding(t, act)
+
+        @pl.when(t // 2 == tm)
+        def _():
+            for kind in range(2):
+                wait(three_parts(kind), ysend.at[lax.rem(t, 2), kind])
+                wait(whole(t, kind), sibsend.at[t, kind])
 
         @pl.when(t // 2 != tm)
         def _():
@@ -293,8 +301,6 @@
     for s in range(2):
         @pl.when(jnp.logical_or(tm != 0, s == 1))
         def _(s=s):
-            wait(ja.at[0, pl.ds(0, 3)], ysend.at[s, 0])
-            wait(ia.at[0, pl.ds(0, 3 * Q)], ysend.at[s, 1])
             for g in range(TM):
                 wait(stage.at[0], out_recv.at[s, g])
 
@@ -335,11 +341,11 @@
             pltpu.VMEM((2, NET, W, BLK), bf16),
             dma((6,)),
             dma((2, 2)),
-            dma((STEPS, COLS, 2)),
+            dma((STEPS, COLS)),
             dma((STEPS, 2)),
             dma((2, 2)),
             dma((STEPS, 2)),
-            dma((STEPS, 2)),
+            dma((STEPS,)),
             dma((TM,)),
             dma((TM,)),
             dma((TM,)),

time: 160 us -> 150 us (0.938)
  Pallas kernels: 158 us -> 148 us
    pallas_call x1, Pallas kernels: 158 us -> 148 us  [local(): pl.pallas_call(kernel, out_shape=jax.ShapeDtypeStruct((2, TM, W, NB * BLK...]
where the time goes in v3:
time: 150 us
  Pallas kernels  148 us (99%)
  local copies, waits for them, and re-layouts  1.77 us (1%)
    pallas_call x1, Pallas kernels, local(): pl.pallas_call(kernel, out_shape=jax.ShapeDtypeStruct((2, TM, W, NB * BLK...  148 us

profile of v3, /device:TPU:25, one launch (start us, length us, event | category | flops | bytes accessed | tf_op | source)
XLA Modules:
  0.0 150.0 jit_solution(12714588151232357374)
XLA Ops:
  0.0 148.2 %shard_map.82 = bf16[2,8,24,512]{3,2,1,0:T(8,128)(2,1)} custom-call(bf16[2,4,3,128,128]{4,3,2,1,0:T(8,128)(2,1)} %jac.1, bf16[2,1,16,128,128]{4,3,2,1,0:T(8,128)(2,1)} %iface.1, s32[2,4]{1,0:T(2,128)} %bitcast.3, s32[1,16]{1,0:T(1,128)} %send_hbm.1, s32[1,16]{1,0:T(1,128)} %recv_hbm.1, s32[1,16]{1,0:T(1,128)} %live_hbm.1, s32[192]{0:T(256)} %node_hbm.1, ...), custom_call_target="tpu_custom_call" | custom-call | tf_op jit(solution)/shard_map/pallas_call | solution.py:321
  148.2 1.8 %copy.10 = bf16[2,192,512]{2,1,0:T(8,128)(2,1)} copy(bf16[2,192,512]{2,1,0:T(8,128)(2,1)} %bitcast.2) | data formatting | bytes 786432

commit v4 on v3

--- a/solution.py
+++ b/solution.py
@@ -28,9 +28,9 @@
 
 def kernel(
     jac, iface, bcols_hbm, send_hbm, recv_hbm, live_hbm, node_hbm, gain_hbm, out,
-    ja, ia, bcols, send, recv, live, node_row, gains, state, zero, wide, wide_out, stage, sbuf, rbuf,
+    ja, ia, bcols, send, recv, live, node_row, gains, meta, state, zero, wide, wide_out, node_cols, gain_cols, first, acc, stage, sbuf, rbuf,
     small_sem, own_sem, quarter_sem, sib_sem, ysend, sibsend, xsend,
-    gain_send, gain_recv, first_send, first_recv,
+    gain_send, gain_recv, meta_send, meta_recv, first_send, first_recv,
     ex_send, ex_recv, out_send, out_recv,
 ):
     tm = lax.axis_index("tm")
@@ -61,7 +61,7 @@
         pltpu.make_async_copy(src, dst, small_sem.at[n])
         for n, (src, dst) in enumerate((
             (bcols_hbm, bcols), (send_hbm, send), (recv_hbm, recv), (live_hbm, live),
-            (node_hbm, node_row), (gain_hbm, gains.at[tm]),
+            (node_hbm, node_row), (gain_hbm, gains.at[tm]), (send_hbm, meta.at[me]),
         ))
     ]
     for s in range(2):
@@ -86,21 +86,25 @@
             for i, total in enumerate(sums)
         ]
 
-    wide_lane = lax.broadcasted_iota(jnp.int32, (W, WIDE), 1)
-    wide_row = lax.broadcasted_iota(jnp.int32, (W, WIDE), 0)
-
-    def column(row, g):
-        picked = jnp.where(wide_lane == wide_row + g * W, row, jnp.zeros_like(row))
-        return jnp.broadcast_to(jnp.sum(picked, axis=1, keepdims=True), (W, BLK))
-
-    def nodes_of(g):
-        return column(node_row[...].reshape(1, WIDE).astype(jnp.float32), g).astype(jnp.int32)
+    def column(row, start, rows):
+        at = lax.broadcasted_iota(jnp.int32, (rows, WIDE), 1) == start + lax.broadcasted_iota(jnp.int32, (rows, WIDE), 0)
+        picked = jnp.where(at, row, jnp.zeros_like(row))
+        return jnp.broadcast_to(jnp.sum(picked, axis=1, keepdims=True), (rows, BLK))
+
+    def nodes_of(start, rows):
+        return column(node_row[...].reshape(1, WIDE).astype(jnp.float32), start, rows).astype(jnp.int32)
 
     def inject(total, i, nodes, gain_rows):
         return total + jnp.where(nodes == lane + (me * NB + i) * BLK, gain_rows, 0.0)
 
     for copy in own:
         copy.wait()
+
+    def keep_wide(s, i, total):
+        for g in range(TM):
+            new = total[g * W : (g + 1) * W].astype(jnp.bfloat16)
+            wide[g, i] = new
+            wide_out[s, g, :, i * BLK : (i + 1) * BLK] = new
 
     @pl.when(tm == 0)
     def _():
@@ -108,21 +112,21 @@
         sums = near_terms(0, zero)
         for q in range(NET):
             sums = add_interface(sums, 0, q, zero[0])
-        for g in range(TM):
-            nodes, gain_rows = nodes_of(g), column(gains[0, 0:1], g)
-            for i in range(NB):
-                new = inject(sums[i], i, nodes, gain_rows).astype(jnp.bfloat16)
-                wide[g, i] = new
-                wide_out[g, :, i * BLK : (i + 1) * BLK] = new
-        pltpu.make_async_copy(wide_out, out.at[0], out_recv.at[0, 0]).start()
-        state[...] = wide[0]
+        node_cols[...] = nodes_of(0, WIDE)
+        for s in range(2):
+            gain_cols[s] = column(gains[0, s : s + 1], 0, WIDE)
+        for i in range(NB):
+            total = inject(jnp.concatenate([sums[i]] * TM, axis=0), i, node_cols[...], gain_cols[0])
+            first[i] = total.astype(jnp.bfloat16)
+            keep_wide(0, i, total)
+        pltpu.make_async_copy(wide_out.at[0], out.at[0], out_recv.at[0, 0]).start()
 
     pl.semaphore_wait(barrier, NET - 1 + TM - 1 + COLS - 1)
 
     @pl.when(tm == 0)
     def _():
-        for g in range(1, TM):
-            remote(wide.at[g], state, first_send.at[g], first_recv, tm=g).start()
+        for d in FAR:
+            remote(send_hbm, meta.at[me], meta_send.at[d], meta_recv.at[d], net=lax.rem(me + d, NET)).start()
 
     def part(t, k, kind):
         return ja.at[t, k] if kind == 0 else ia.at[t, pl.ds(k * Q, Q)]
@@ -183,15 +187,35 @@
         def _():
             spread_own(t)
 
-    spread(1)
+    spread(2)
 
     for d in range(1, TM):
         there = lax.rem(tm + d, TM)
         remote(gain_hbm, gains.at[tm], gain_send.at[d], gain_recv.at[d], tm=there).start()
 
-    @pl.when(tm != 0)
-    def _():
-        wait(state, first_recv)
+    @pl.when(tm == 0)
+    def _():
+        for i, total in enumerate(near_terms(1, first)):
+            acc[i] = inject(total, i, node_cols[...], gain_cols[1])
+        for d in FAR:
+            wait(meta.at[0], meta_recv.at[d])
+
+        def add(q, carry):
+            mine = lax.broadcasted_iota(jnp.int32, (1, NET), 1) == me
+            block = jnp.sum(jnp.where(mine, meta[q].astype(jnp.float32), 0.0), axis=1, keepdims=True)
+            base = (q * NB + block.astype(jnp.int32)) * BLK
+            values = jnp.where(node_cols[...] == lane + base, gain_cols[0], 0.0).astype(jnp.bfloat16)
+            for i, total in enumerate(add_interface([acc[i] for i in range(NB)], 1, q, values)):
+                acc[i] = total
+            return carry
+
+        lax.fori_loop(0, NET, add, 0)
+        for i in range(NB):
+            keep_wide(1, i, acc[i])
+        for g in range(1, TM):
+            remote(wide.at[g], state, first_send.at[g], first_recv, tm=g).start()
+        state[...] = wide[0]
+        pltpu.make_async_copy(wide_out.at[1], out.at[1], out_recv.at[1, 0]).start()
 
     def exchange(t):
         slot = lax.rem(t, 2)
@@ -215,52 +239,32 @@
         for d in FAR:
             wait(sbuf.at[slot, d], ex_send.at[slot, d])
 
-    nodes = nodes_of(tm)
+    nodes = nodes_of(tm * W, W)
+    for d in range(1, TM):
+        wait(gains.at[lax.rem(tm - d + TM, TM)], gain_recv.at[d])
+    spread(3)
+    forward_own_quarter(2)
+
+    @pl.when(tm != 0)
+    def _():
+        wait(state, first_recv)
+
 
     def step(t, carry):
         slot = lax.rem(t, 2)
         exchange(t)
 
-        @pl.when(t > 1)
+        @pl.when(t > 2)
         def _():
             output(t - 1)
             sent(1 - slot)
 
-        @pl.when(t == 1)
-        def _():
-            spread(2)
-            forward_own_quarter(1)
-            forward_other_quarters(1)
-            forward_own_quarter(2)
-            for d in range(1, TM):
-                wait(gains.at[lax.rem(tm - d + TM, TM)], gain_recv.at[d])
-
-        @pl.when(t == 2)
-        def _():
-            forward_other_quarters(2)
-            forward_own_quarter(3)
-
-        @pl.when(t == 3)
-        def _():
-            forward_other_quarters(3)
-
-        @pl.when(t >= 2)
-        def _():
-            spread(t + 3)
-            forward_own_quarter(t + 2)
-
-        @pl.when(t >= 3)
-        def _():
-            forward_other_quarters(t + 1)
-
+        forward_own_quarter(t + 1)
+        forward_other_quarters(t)
+        spread(t + 2)
         from_sibling(t)
 
-        @pl.when(t == 1)
-        def _():
-            spread(3)
-            spread(4)
-
-        gain_rows = column(gains[t // 2, pl.ds(lax.rem(t, 2), 1)], tm)
+        gain_rows = column(gains[t // 2, pl.ds(lax.rem(t, 2), 1)], tm * W, W)
         sums = [inject(total, i, nodes, gain_rows) for i, total in enumerate(near_terms(t, state))]
         sums = add_interface(sums, t, me, state[send[0, me]])
         for group in GROUPS:
@@ -274,7 +278,7 @@
             stage[t, :, i * BLK : (i + 1) * BLK] = new
         return carry
 
-    lax.fori_loop(1, STEPS, step, 0)
+    lax.fori_loop(2, STEPS, step, 0)
     output(STEPS - 1)
     sent((STEPS - 1) % 2)
 
@@ -297,10 +301,10 @@
 
         return carry
 
-    lax.fori_loop(1, STEPS, drain, 0)
-    for s in range(2):
-        @pl.when(jnp.logical_or(tm != 0, s == 1))
-        def _(s=s):
+    lax.fori_loop(2, STEPS, drain, 0)
+    @pl.when(tm != 0)
+    def _():
+        for s in range(2):
             for g in range(TM):
                 wait(stage.at[0], out_recv.at[s, g])
 
@@ -309,9 +313,12 @@
 
     @pl.when(tm == 0)
     def _():
-        pltpu.make_async_copy(wide_out, out.at[0], out_recv.at[0, 0]).wait()
+        for s in range(2):
+            pltpu.make_async_copy(wide_out.at[s], out.at[s], out_recv.at[s, 0]).wait()
         for g in range(1, TM):
             wait(state, first_send.at[g])
+        for d in FAR:
+            wait(meta.at[0], meta_send.at[d])
 
 
 def local(jac, block_cols, iface_jac, iface_send, iface_recv, iface_live, ctrl_node, ctrl_gain):
@@ -332,14 +339,19 @@
             pltpu.SMEM((1, NET), i32),
             pltpu.VMEM((WIDE,), i32),
             pltpu.VMEM((TM, 2, WIDE), f32),
+            pltpu.VMEM((NET, 1, NET), i32),
             pltpu.VMEM((NB, W, BLK), bf16),
             pltpu.VMEM((NB, W, BLK), bf16),
             pltpu.VMEM((TM, NB, W, BLK), bf16),
-            pltpu.VMEM((TM, W, NB * BLK), bf16),
+            pltpu.VMEM((2, TM, W, NB * BLK), bf16),
+            pltpu.VMEM((WIDE, BLK), i32),
+            pltpu.VMEM((2, WIDE, BLK), f32),
+            pltpu.VMEM((NB, WIDE, BLK), bf16),
+            pltpu.VMEM((NB, WIDE, BLK), f32),
             pltpu.VMEM((STEPS, W, NB * BLK), bf16),
             pltpu.VMEM((2, NET, W, BLK), bf16),
             pltpu.VMEM((2, NET, W, BLK), bf16),
-            dma((6,)),
+            dma((7,)),
             dma((2, 2)),
             dma((STEPS, COLS)),
             dma((STEPS, 2)),
@@ -348,6 +360,8 @@
             dma((STEPS,)),
             dma((TM,)),
             dma((TM,)),
+            dma((NET,)),
+            dma((NET,)),
             dma((TM,)),
             dma,
             dma((2, NET)),

time: 150 us -> 139 us (0.927)
  Pallas kernels: 148 us -> 137 us
    pallas_call x1, Pallas kernels: 148 us -> 137 us  [local(): pl.pallas_call(kernel, out_shape=jax.ShapeDtypeStruct((2, TM, W, NB * BLK...]
where the time goes in v4:
time: 139 us
  Pallas kernels  137 us (99%)
  local copies, waits for them, and re-layouts  1.77 us (1%)
    pallas_call x1, Pallas kernels, local(): pl.pallas_call(kernel, out_shape=jax.ShapeDtypeStruct((2, TM, W, NB * BLK...  137 us

profile of v4, /device:TPU:25, one launch (start us, length us, event | category | flops | bytes accessed | tf_op | source)
XLA Modules:
  0.0 139.1 jit_solution(12930073498408845254)
XLA Ops:
  0.0 137.3 %shard_map.82 = bf16[2,8,24,512]{3,2,1,0:T(8,128)(2,1)} custom-call(bf16[2,4,3,128,128]{4,3,2,1,0:T(8,128)(2,1)} %jac.1, bf16[2,1,16,128,128]{4,3,2,1,0:T(8,128)(2,1)} %iface.1, s32[2,4]{1,0:T(2,128)} %bitcast.3, s32[1,16]{1,0:T(1,128)} %send_hbm.1, s32[1,16]{1,0:T(1,128)} %recv_hbm.1, s32[1,16]{1,0:T(1,128)} %live_hbm.1, s32[192]{0:T(256)} %node_hbm.1, ...), custom_call_target="tpu_custom_call" | custom-call | tf_op jit(solution)/shard_map/pallas_call | solution.py:328
  137.3 1.8 %copy.10 = bf16[2,192,512]{2,1,0:T(8,128)(2,1)} copy(bf16[2,192,512]{2,1,0:T(8,128)(2,1)} %bitcast.2) | data formatting | bytes 786432

commit v5 on v4

--- a/solution.py
+++ b/solution.py
@@ -17,7 +17,7 @@
 Q = NET // COLS
 NEAR = sorted(range(1, NET), key=lambda d: min(d, NET - d))
 FAR = NEAR[::-1]
-GROUPS = (NEAR[:8], NEAR[8:])
+GROUPS = (NEAR[:10], NEAR[10:])
 
 
 def dot_t(x, w):
@@ -28,7 +28,7 @@
 
 def kernel(
     jac, iface, bcols_hbm, send_hbm, recv_hbm, live_hbm, node_hbm, gain_hbm, out,
-    ja, ia, bcols, send, recv, live, node_row, gains, meta, state, zero, wide, wide_out, node_cols, gain_cols, first, acc, stage, sbuf, rbuf,
+    ja, ia, bcols, send, recv, live, node_row, gains, meta, state, pair, zero, wide, wide_out, node_cols, gain_cols, first, acc, stage, sbuf, rbuf,
     small_sem, own_sem, quarter_sem, sib_sem, ysend, sibsend, xsend,
     gain_send, gain_recv, meta_send, meta_recv, first_send, first_recv,
     ex_send, ex_recv, out_send, out_recv,
@@ -100,11 +100,20 @@
     for copy in own:
         copy.wait()
 
-    def keep_wide(s, i, total):
-        for g in range(TM):
-            new = total[g * W : (g + 1) * W].astype(jnp.bfloat16)
-            wide[g, i] = new
-            wide_out[s, g, :, i * BLK : (i + 1) * BLK] = new
+    def rows_of(total, g):
+        return total[g * W : (g + 1) * W]
+
+    def matches(nodes):
+        mine = lax.broadcasted_iota(jnp.int32, (1, NET), 1) == me
+        hit = jnp.zeros(nodes.shape, jnp.float32)
+        for q in range(NET):
+            block = jnp.sum(jnp.where(mine, meta[q].astype(jnp.float32), 0.0), axis=1, keepdims=True)
+            offset = nodes - (q * NB + block.astype(jnp.int32)) * BLK
+            hit = jnp.where(jnp.logical_and(offset >= 0, offset < BLK), 1.0, hit)
+        return hit
+
+    def pick(hit, there, otherwise):
+        return jnp.where(hit > 0.5, there.astype(jnp.float32), otherwise.astype(jnp.float32)).astype(jnp.bfloat16)
 
     @pl.when(tm == 0)
     def _():
@@ -118,15 +127,40 @@
         for i in range(NB):
             total = inject(jnp.concatenate([sums[i]] * TM, axis=0), i, node_cols[...], gain_cols[0])
             first[i] = total.astype(jnp.bfloat16)
-            keep_wide(0, i, total)
+            for g in range(TM):
+                wide_out[0, g, :, i * BLK : (i + 1) * BLK] = rows_of(total, g).astype(jnp.bfloat16)
         pltpu.make_async_copy(wide_out.at[0], out.at[0], out_recv.at[0, 0]).start()
 
+        for i, total in enumerate(near_terms(1, first)):
+            total = inject(total, i, node_cols[...], gain_cols[1])
+            acc[i] = total
+            for g in range(TM):
+                wide[g, 0, i] = rows_of(total, g).astype(jnp.bfloat16)
+
+        def add(q, carry):
+            offset = node_cols[...] - q * NB * BLK
+            inside = jnp.logical_and(offset >= 0, offset < NB * BLK)
+            here = jnp.logical_and(inside, jnp.bitwise_and(offset, BLK - 1) == lane)
+            values = jnp.where(here, gain_cols[0], 0.0).astype(jnp.bfloat16)
+            for i, total in enumerate(add_interface([acc[i] for i in range(NB)], 1, q, values)):
+                acc[i] = total
+            return carry
+
+        lax.fori_loop(0, NET, add, 0)
+        for i in range(NB):
+            for g in range(TM):
+                wide[g, 1, i] = acc[i, g * W : (g + 1) * W].astype(jnp.bfloat16)
+
     pl.semaphore_wait(barrier, NET - 1 + TM - 1 + COLS - 1)
+
+    for d in FAR:
+        remote(send_hbm, meta.at[me], meta_send.at[d], meta_recv.at[d], net=lax.rem(me + d, NET)).start()
 
     @pl.when(tm == 0)
     def _():
-        for d in FAR:
-            remote(send_hbm, meta.at[me], meta_send.at[d], meta_recv.at[d], net=lax.rem(me + d, NET)).start()
+        for g in range(1, TM):
+            remote(wide.at[g], pair, first_send.at[g], first_recv, tm=g).start()
+        pair[...] = wide[0]
 
     def part(t, k, kind):
         return ja.at[t, k] if kind == 0 else ia.at[t, pl.ds(k * Q, Q)]
@@ -193,30 +227,6 @@
         there = lax.rem(tm + d, TM)
         remote(gain_hbm, gains.at[tm], gain_send.at[d], gain_recv.at[d], tm=there).start()
 
-    @pl.when(tm == 0)
-    def _():
-        for i, total in enumerate(near_terms(1, first)):
-            acc[i] = inject(total, i, node_cols[...], gain_cols[1])
-        for d in FAR:
-            wait(meta.at[0], meta_recv.at[d])
-
-        def add(q, carry):
-            mine = lax.broadcasted_iota(jnp.int32, (1, NET), 1) == me
-            block = jnp.sum(jnp.where(mine, meta[q].astype(jnp.float32), 0.0), axis=1, keepdims=True)
-            base = (q * NB + block.astype(jnp.int32)) * BLK
-            values = jnp.where(node_cols[...] == lane + base, gain_cols[0], 0.0).astype(jnp.bfloat16)
-            for i, total in enumerate(add_interface([acc[i] for i in range(NB)], 1, q, values)):
-                acc[i] = total
-            return carry
-
-        lax.fori_loop(0, NET, add, 0)
-        for i in range(NB):
-            keep_wide(1, i, acc[i])
-        for g in range(1, TM):
-            remote(wide.at[g], state, first_send.at[g], first_recv, tm=g).start()
-        state[...] = wide[0]
-        pltpu.make_async_copy(wide_out.at[1], out.at[1], out_recv.at[1, 0]).start()
-
     def exchange(t):
         slot = lax.rem(t, 2)
         for d in FAR:
@@ -240,14 +250,18 @@
             wait(sbuf.at[slot, d], ex_send.at[slot, d])
 
     nodes = nodes_of(tm * W, W)
-    for d in range(1, TM):
-        wait(gains.at[lax.rem(tm - d + TM, TM)], gain_recv.at[d])
+    forward_own_quarter(2)
     spread(3)
-    forward_own_quarter(2)
 
     @pl.when(tm != 0)
     def _():
-        wait(state, first_recv)
+        wait(pair, first_recv)
+
+    for d in FAR:
+        wait(meta.at[0], meta_recv.at[d])
+    hit = matches(nodes)
+    for i in range(NB):
+        state[i] = pick(hit, pair[1, i], pair[0, i])
 
 
     def step(t, carry):
@@ -258,11 +272,24 @@
         def _():
             output(t - 1)
             sent(1 - slot)
+
+        @pl.when(jnp.logical_and(t == 2, tm == 0))
+        def _():
+            hits = matches(node_cols[...])
+            for i in range(NB):
+                for g in range(TM):
+                    wide_out[1, g, :, i * BLK : (i + 1) * BLK] = pick(rows_of(hits, g), wide[g, 1, i], wide[g, 0, i])
+            pltpu.make_async_copy(wide_out.at[1], out.at[1], out_recv.at[1, 0]).start()
 
         forward_own_quarter(t + 1)
         forward_other_quarters(t)
         spread(t + 2)
         from_sibling(t)
+
+        @pl.when(t == 2)
+        def _():
+            for d in range(1, TM):
+                wait(gains.at[lax.rem(tm - d + TM, TM)], gain_recv.at[d])
 
         gain_rows = column(gains[t // 2, pl.ds(lax.rem(t, 2), 1)], tm * W, W)
         sums = [inject(total, i, nodes, gain_rows) for i, total in enumerate(near_terms(t, state))]
@@ -316,9 +343,10 @@
         for s in range(2):
             pltpu.make_async_copy(wide_out.at[s], out.at[s], out_recv.at[s, 0]).wait()
         for g in range(1, TM):
-            wait(state, first_send.at[g])
-        for d in FAR:
-            wait(meta.at[0], meta_send.at[d])
+            wait(pair, first_send.at[g])
+
+    for d in FAR:
+        wait(meta.at[0], meta_send.at[d])
 
 
 def local(jac, block_cols, iface_jac, iface_send, iface_recv, iface_live, ctrl_node, ctrl_gain):
@@ -341,8 +369,9 @@
             pltpu.VMEM((TM, 2, WIDE), f32),
             pltpu.VMEM((NET, 1, NET), i32),
             pltpu.VMEM((NB, W, BLK), bf16),
+            pltpu.VMEM((2, NB, W, BLK), bf16),
             pltpu.VMEM((NB, W, BLK), bf16),
-            pltpu.VMEM((TM, NB, W, BLK), bf16),
+            pltpu.VMEM((TM, 2, NB, W, BLK), bf16),
             pltpu.VMEM((2, TM, W, NB * BLK), bf16),
             pltpu.VMEM((WIDE, BLK), i32),
             pltpu.VMEM((2, WIDE, BLK), f32),

time: 139 us -> 137 us (0.986)
  no operation moved by 1% of the time
where the time goes in v5:
time: 137 us; the launch traced here: 138 us
  Pallas kernels  136 us (99%)
  local copies, waits for them, and re-layouts  1.77 us (1%)
    pallas_call x1, Pallas kernels, local(): pl.pallas_call(kernel, out_shape=jax.ShapeDtypeStruct((2, TM, W, NB * BLK...  136 us

profile of v5, /device:TPU:25, one launch (start us, length us, event | category | flops | bytes accessed | tf_op | source)
XLA Modules:
  0.0 138.2 jit_solution(6539058166003593499)
XLA Ops:
  0.0 136.4 %shard_map.82 = bf16[2,8,24,512]{3,2,1,0:T(8,128)(2,1)} custom-call(bf16[2,4,3,128,128]{4,3,2,1,0:T(8,128)(2,1)} %jac.1, bf16[2,1,16,128,128]{4,3,2,1,0:T(8,128)(2,1)} %iface.1, s32[2,4]{1,0:T(2,128)} %bitcast.3, s32[1,16]{1,0:T(1,128)} %send_hbm.1, s32[1,16]{1,0:T(1,128)} %recv_hbm.1, s32[1,16]{1,0:T(1,128)} %live_hbm.1, s32[192]{0:T(256)} %node_hbm.1, ...), custom_call_target="tpu_custom_call" | custom-call | tf_op jit(solution)/shard_map/pallas_call | solution.py:356
  136.4 1.8 %copy.10 = bf16[2,192,512]{2,1,0:T(8,128)(2,1)} copy(bf16[2,192,512]{2,1,0:T(8,128)(2,1)} %bitcast.2) | data formatting | bytes 786432

commit v6 on v5

--- a/solution.py
+++ b/solution.py
@@ -97,8 +97,11 @@
     def inject(total, i, nodes, gain_rows):
         return total + jnp.where(nodes == lane + (me * NB + i) * BLK, gain_rows, 0.0)
 
-    for copy in own:
-        copy.wait()
+    def own_arrived():
+        for copy in own:
+            copy.wait()
+
+    pl.when(tm == 0)(own_arrived)
 
     def rows_of(total, g):
         return total[g * W : (g + 1) * W]
@@ -249,6 +252,7 @@
         for d in FAR:
             wait(sbuf.at[slot, d], ex_send.at[slot, d])
 
+    pl.when(tm != 0)(own_arrived)
     nodes = nodes_of(tm * W, W)
     forward_own_quarter(2)
     spread(3)

time: 137 us -> 137 us (level)
  no operation moved by 1% of the time
where the time goes in v6:
time: 137 us; the launch traced here: 138 us
  Pallas kernels  136 us (99%)
  local copies, waits for them, and re-layouts  1.77 us (1%)
    pallas_call x1, Pallas kernels, local(): pl.pallas_call(kernel, out_shape=jax.ShapeDtypeStruct((2, TM, W, NB * BLK...  136 us

profile of v6, /device:TPU:25, one launch (start us, length us, event | category | flops | bytes accessed | tf_op | source)
XLA Modules:
  0.0 137.9 jit_solution(7284572758348241063)
XLA Ops:
  0.0 136.1 %shard_map.82 = bf16[2,8,24,512]{3,2,1,0:T(8,128)(2,1)} custom-call(bf16[2,4,3,128,128]{4,3,2,1,0:T(8,128)(2,1)} %jac.1, bf16[2,1,16,128,128]{4,3,2,1,0:T(8,128)(2,1)} %iface.1, s32[2,4]{1,0:T(2,128)} %bitcast.3, s32[1,16]{1,0:T(1,128)} %send_hbm.1, s32[1,16]{1,0:T(1,128)} %recv_hbm.1, s32[1,16]{1,0:T(1,128)} %live_hbm.1, s32[192]{0:T(256)} %node_hbm.1, ...), custom_call_target="tpu_custom_call" | custom-call | tf_op jit(solution)/shard_map/pallas_call | solution.py:360
  136.1 1.8 %copy.10 = bf16[2,192,512]{2,1,0:T(8,128)(2,1)} copy(bf16[2,192,512]{2,1,0:T(8,128)(2,1)} %bitcast.2) | data formatting | bytes 786432
